TPU v7x, 32 devices: a whole 2x2x4 slice. The times are simulated.
32 devices in a mesh: row: 4 (over z), col: 8 (over y, x, core).
Axes of the slice: x: 2, y: 2, z: 4, core: 2. Of those that a mesh axis runs over, the one named last changes fastest.
Arguments:
- amplitudes: bfloat16 [16, 16, 12, 4096], P('row', 'col'), may hold values from -6 to 6
- integrals: bfloat16 [16, 16, 47, 4096], P('row', 'col'), may hold values from -0.1875 to 0.1875
- pair_lists: int32 [4, 12, 2], replicated, may hold values from 0 to 46, as said below
- tile_counts: int32 [4], replicated, may hold values from 1 to 12, as said below
Outputs:
- symmetric: float32 [16, 16, 12, 4096], P('row', 'col')
Inputs may be any that keep to these rules, and one draw needn't show every extreme that they name: `pair_lists`: each grid row lists 12 distinct ordered pairs of different tiles. `tile_counts`: the largest count equals 12.
All inputs are finite; a program needn't handle non-finite values.
Results may differ from a plain program's by a relative error of at most 0.0029.
Values may be sent and summed in bfloat16 or wider, within the bound.
No kernel may reach another device: no remote copies, remote signals or barrier semaphores. Data moves between devices by JAX's collectives and lax.ppermute only.
A program may use at most 128 MiB of HBM per device.

v0:
```python
import jax
import jax.numpy as jnp
from jax import lax
from jax.sharding import PartitionSpec as P

TILE = 64


def on_device(amplitudes, integrals, pair_lists, tile_counts):
    occ_row, occ_col, slot_count, square = amplitudes.shape
    tile_width = TILE
    row_devices = lax.axis_size("row")
    col_devices = lax.axis_size("col")
    col_ratio = col_devices // row_devices
    my_row = lax.axis_index("row")
    my_col = lax.axis_index("col")
    partner_row = my_col // col_ratio
    tile_first = pair_lists[:, :, 0]
    tile_second = pair_lists[:, :, 1]
    packed = jnp.take(integrals, tile_second.reshape(-1), axis=2)
    packed = packed.reshape(occ_row, occ_col, row_devices, slot_count, square)
    received = lax.all_to_all(packed, "row", split_axis=2, concat_axis=0, tiled=True)
    received = received.reshape(occ_row * row_devices, occ_col, slot_count, square)
    piece = lax.all_gather(amplitudes, "col", axis=1, tiled=True)
    piece_count = piece.shape[1]
    left_tiles = piece.reshape(occ_row, piece_count, slot_count, tile_width, tile_width)
    right_tiles = received.reshape(piece_count, occ_col, slot_count, tile_width, tile_width)
    cycle_sum = jnp.einsum(
        "iksac,kjscb->ijsab", left_tiles, right_tiles, preferred_element_type=jnp.float32
    )
    my_count = lax.dynamic_index_in_dim(tile_counts, my_row, 0, keepdims=False)
    live_slots = (jnp.arange(slot_count, dtype=jnp.int32) < my_count).astype(jnp.float32)
    cycle_value = (cycle_sum * live_slots[None, None, :, None, None]).astype(jnp.bfloat16)
    cycle = cycle_value.reshape(occ_row, occ_col, slot_count, square)
    residual_strip = lax.all_gather(cycle, "row", axis=0, tiled=True)
    mirror_whole = lax.all_to_all(residual_strip, "col", split_axis=0, concat_axis=1, tiled=True)
    mirror_block = lax.dynamic_slice_in_dim(mirror_whole, my_row * occ_row, occ_row, 1)
    mirror_block = mirror_block.reshape(occ_col, occ_row, slot_count, tile_width, tile_width)
    mine_first = lax.dynamic_index_in_dim(tile_first, my_row, 0, keepdims=False)
    mine_second = lax.dynamic_index_in_dim(tile_second, my_row, 0, keepdims=False)
    their_first = lax.dynamic_index_in_dim(tile_first, partner_row, 0, keepdims=False)
    their_second = lax.dynamic_index_in_dim(tile_second, partner_row, 0, keepdims=False)
    pair_match = (
        (mine_first[:, None] == their_second[None, :])
        & (mine_second[:, None] == their_first[None, :])
    ).astype(jnp.bfloat16)
    crossed = jnp.einsum(
        "st,jitba->ijsab", pair_match, mirror_block, preferred_element_type=jnp.float32
    )
    own_part = cycle_value.astype(jnp.float32)
    symmetric = (own_part + crossed) * live_slots[None, None, :, None, None]
    return symmetric.reshape(occ_row, occ_col, slot_count, square)


def solution(mesh):
    return jax.shard_map(
        on_device,
        mesh=mesh,
        in_specs=(P("row", "col", None, None), P("row", "col", None, None), P(), P()),
        out_specs=P("row", "col", None, None),
        check_vma=False,
    )
```

profile of v0, /device:TPU:3, one launch (start us, length us, event | category | flops | bytes accessed | tf_op | source)
XLA Modules:
  0.0 286.2 jit_solution(7167490492308642510)
XLA Ops:
  6.5 0.0 copy-start
  6.5 0.0 all-gather.3.cloned.1.call-start
  6.5 2.8 copy.17
  9.3 0.0 all-gather.3.cloned.1.call-update
  9.3 0.8 fusion.29
  10.1 0.1 reshape_squeeze.6
  10.2 0.0 copy-done
  10.2 8.5 %gather_fusion = bf16[48,4,2,4096]{3,2,1,0:T(2,128)(2,1)} fusion(bf16[4,2,47,4096]{3,1,2,0:T(2,128)(2,1)S(1)} %copy-done, s32[1024]{0:T(1024)S(1)} %pad_clamp_fusion), kind=kCustom, calls=%fused_computation | custom fusion | bytes 6291648 | tf_op jit(solution)/shard_map/jit(_take)/gather | solution.py:20
  18.8 6.6 %broadcast_select_fusion = bf16[4,2,4,12,4096]{4,1,3,0,2:T(2,128)(2,1)} fusion(pred[4,12]{1,0:T(4,128)(4,1)S(1)} %compare_and_fusion, bf16[4,2,4,12,4096]{4,1,0,3,2:T(2,128)(2,1)} %bitcast.67), kind=kLoop, calls=%fused_computation.4 | loop fusion | flops 1572864 | bytes 6291504 | tf_op jit(solution)/shard_map/jit(_take)/select_n | solution.py:20
  25.4 0.0 copy-start.4
  25.4 4.8 %all-to-all-start = ((bf16[4,2,4,12,4096]{4,1,3,0,2:T(2,128)(2,1)}), bf16[4,2,4,12,4096]{4,1,3,0,2:T(2,128)(2,1)}, u32[]{:S(2)}, u32[]{:S(2)}) async-start(bf16[4,2,4,12,4096]{4,1,3,0,2:T(2,128)(2,1)} %broadcast_select_fusion), calls=%async_computation | async-start | bytes 6291456 | tf_op jit(solution)/shard_map/all_to_all | solution.py:22
  30.2 0.2 all-gather.5.cloned.1.call-start
  30.4 0.0 copy-done.4
  30.4 0.6 dynamic_slice.20
  31.1 0.6 compare_convert_fusion
  31.7 68.8 %all-to-all-done = bf16[4,2,4,12,4096]{4,1,3,0,2:T(2,128)(2,1)} async-done(((bf16[4,2,4,12,4096]{4,1,3,0,2:T(2,128)(2,1)}), bf16[4,2,4,12,4096]{4,1,3,0,2:T(2,128)(2,1)}, u32[]{:S(2)}, u32[]{:S(2)}) %all-to-all-start) | async-done | bytes 3145760 | tf_op jit(solution)/shard_map/all_to_all | solution.py:22
  100.4 11.1 %reshape_reshape.3 = bf16[16,2,12,64,64]{4,3,1,2,0:T(8,128)(2,1)} reshape(bf16[4,4,2,1,12,4096]{5,2,4,1,0,3:T(2,128)(2,1)} %bitcast.5) | data formatting | bytes 6291456 | tf_op jit(solution)/shard_map/reshape;reshape | solution.py:27
  111.5 0.0 all-gather.3.cloned.1.call-done
  111.5 9.4 %copy.18 = bf16[4,16,12,4096]{3,1,0,2:T(8,128)(2,1)} copy(bf16[4,16,12,4096]{3,0,2,1:T(4,128)(2,1)} %all-gather.3.cloned.1.call-done) | data formatting | bytes 12582912 | tf_op jit(solution)/shard_map/all_gather | solution.py:24
  120.9 17.9 %reshape.81 = bf16[4,16,12,64,64,1]{4,3,1,0,2,5:T(8,128)(2,1)} reshape(bf16[4,16,12,4096]{3,1,0,2:T(8,128)(2,1)} %copy.18) | data formatting | bytes 12582912 | tf_op jit(solution)/shard_map/reshape | solution.py:26
  138.8 11.1 %fusion.11 = bf16[4,2,12,64,64]{3,4,0,1,2:T(8,128)(2,1)S(1)} fusion(f32[12]{0:T(128)S(1)} %compare_convert_fusion, bf16[4,16,12,64,64,1]{4,3,1,0,2,5:T(8,128)(2,1)} %reshape.81, bf16[16,2,12,64,64]{4,3,1,2,0:T(8,128)(2,1)} %reshape_reshape.3), kind=kOutput, calls=%fused_computation.11 | convolution fusion | flops 806092800 | bytes 10223664 | tf_op jit(solution)/shard_map/iksac,kjscb->ijsab/dot_general | solution.py:28
  149.9 0.0 copy-start.2
  149.9 1.7 copy.20
  151.6 3.9 %reshape.69 = bf16[4,2,12,4096]{3,1,2,0:T(2,128)(2,1)} reshape(bf16[4,2,12,64,64]{4,3,1,2,0:T(8,128)(2,1)} %copy.20) | data formatting | bytes 1572864 | tf_op jit(solution)/shard_map/reshape | solution.py:34
  155.4 0.0 all-gather.5.cloned.1.call-update
  155.5 0.0 copy-done.2
  155.5 63.3 %all-gather.5.cloned.1.call-done = bf16[16,2,12,4096]{3,1,2,0:T(2,128)(2,1)} async-done(((bf16[4,2,12,4096]{3,1,2,0:T(2,128)(2,1)}), bf16[16,2,12,4096]{3,1,2,0:T(2,128)(2,1)}) %all-gather.5.cloned.1.call-update) | async-done | bytes 3145744 | tf_op jit(solution)/shard_map/all_gather | solution.py:35
  218.8 5.3 %all-to-all-start.1 = ((bf16[16,2,12,4096]{3,1,2,0:T(2,128)(2,1)}), bf16[16,2,12,4096]{3,1,2,0:T(2,128)(2,1)}, u32[]{:S(2)}, u32[]{:S(2)}) async-start(bf16[16,2,12,4096]{3,1,2,0:T(2,128)(2,1)} %all-gather.5.cloned.1.call-done), calls=%async_computation.1 | async-start | bytes 6291456 | tf_op jit(solution)/shard_map/all_to_all | solution.py:36
  224.1 36.4 %all-to-all-done.1 = bf16[16,2,12,4096]{3,1,2,0:T(2,128)(2,1)} async-done(((bf16[16,2,12,4096]{3,1,2,0:T(2,128)(2,1)}), bf16[16,2,12,4096]{3,1,2,0:T(2,128)(2,1)}, u32[]{:S(2)}, u32[]{:S(2)}) %all-to-all-start.1) | async-done | bytes 3145760 | tf_op jit(solution)/shard_map/all_to_all | solution.py:36
  260.5 5.1 %copy.21 = bf16[8,2,2,12,4096]{4,1,3,2,0:T(2,128)(2,1)S(1)} copy(bf16[8,2,2,12,4096]{4,2,3,1,0:T(2,128)(2,1)} %bitcast.12) | data formatting | bytes 6291456 | tf_op jit(solution)/shard_map/all_to_all | solution.py:36
  265.6 0.7 constant_dynamic-slice_fusion.4
  266.3 1.0 reshape.85
  267.4 0.0 copy-start.3
  267.4 1.1 fusion.5
  268.5 0.3 copy-done.3
  268.8 2.7 fusion.3
  271.5 0.0 copy-start.1
  271.5 3.7 %copy.25 = f32[4,2,12,64,64]{4,3,1,2,0:T(8,128)} copy(f32[4,2,12,64,64]{3,4,0,1,2:T(8,128)} %fusion.3) | data formatting | bytes 3145728 | tf_op jit(solution)/shard_map/mul | solution.py:51
  275.2 4.2 %reshape.71 = f32[4,2,12,4096]{3,1,2,0:T(2,128)} reshape(f32[4,2,12,64,64]{4,3,1,2,0:T(8,128)} %copy.25) | data formatting | bytes 3145728 | tf_op jit(solution)/shard_map/reshape | solution.py:52
  279.4 0.0 copy-done.1
  (4 shorter events, 0.0 us)
Async XLA Ops:
  6.5 3.7 %copy-start = (bf16[4,2,47,4096]{3,1,2,0:T(2,128)(2,1)S(1)}, bf16[4,2,47,4096]{3,1,2,0:T(2,128)(2,1)}, u32[]{:S(2)}) copy-start(bf16[4,2,47,4096]{3,1,2,0:T(2,128)(2,1)} %param.5) | copy-start | bytes 9240580
  6.5 105.0 %all-gather.3.cloned.1.call-start = ((), (), s32[]{:S(2)}) async-start(), calls=%async_computation.2 | async-start | bytes 7077888 | tf_op jit(solution)/shard_map/all_gather | solution.py:24
  25.4 5.0 %copy-start.4 = (s32[4]{0:T(128)S(1)}, s32[4]{0:T(128)}, u32[]{:S(2)}) copy-start(s32[4]{0:T(128)} %param.7) | copy-start | bytes 52
  25.4 75.0 %all-to-all-start = ((bf16[4,2,4,12,4096]{4,1,3,0,2:T(2,128)(2,1)}), bf16[4,2,4,12,4096]{4,1,3,0,2:T(2,128)(2,1)}, u32[]{:S(2)}, u32[]{:S(2)}) async-start(bf16[4,2,4,12,4096]{4,1,3,0,2:T(2,128)(2,1)} %broadcast_select_fusion), calls=%async_computation | async-start | bytes 6291456 | tf_op jit(solution)/shard_map/all_to_all | solution.py:22
  30.2 188.6 %all-gather.5.cloned.1.call-start = ((), (), s32[]{:S(2)}) async-start(), calls=%async_computation.3 | async-start | bytes 3932160 | tf_op jit(solution)/shard_map/all_gather | solution.py:35
  149.9 5.6 %copy-start.2 = (bf16[4,2,12,64,64]{3,4,0,1,2:T(8,128)(2,1)}, bf16[4,2,12,64,64]{3,4,0,1,2:T(8,128)(2,1)S(1)}, u32[]{:S(2)}) copy-start(bf16[4,2,12,64,64]{3,4,0,1,2:T(8,128)(2,1)S(1)} %fusion.11) | copy-start | bytes 2359300
  218.8 41.7 %all-to-all-start.1 = ((bf16[16,2,12,4096]{3,1,2,0:T(2,128)(2,1)}), bf16[16,2,12,4096]{3,1,2,0:T(2,128)(2,1)}, u32[]{:S(2)}, u32[]{:S(2)}) async-start(bf16[16,2,12,4096]{3,1,2,0:T(2,128)(2,1)} %all-gather.5.cloned.1.call-done), calls=%async_computation.1 | async-start | bytes 6291456 | tf_op jit(solution)/shard_map/all_to_all | solution.py:36
  267.4 1.4 copy-start.3
  271.5 7.9 %copy-start.1 = (bf16[4,2,47,4096]{3,1,2,0:T(2,128)(2,1)S(1)}, bf16[4,2,47,4096]{3,1,2,0:T(2,128)(2,1)}, u32[]{:S(2)}) copy-start(bf16[4,2,47,4096]{3,1,2,0:T(2,128)(2,1)} %param.5) | copy-start | bytes 9240580
Sparse Core Ops, SparseCore 0:
  9.5 47.0 all-gather.2
  155.6 63.1 all-gather.4
where the time goes:
time: 290 us; the launch traced here: 286 us
  waiting for transfers between devices  168 us (58%)
  local copies, waits for them, and re-layouts  71.7 us (25%)
  between operations  13.5 us (5%)
  matrix products  12.2 us (4%)
  starting transfers between devices  10.4 us (4%)
  other arithmetic  9.96 us (3%)
    all_to_all x1, waiting for transfers between devices, on_device(): lax.all_to_all(packed, 'row', split_axis=2, concat_axis=0, tiled=True)  68.8 us
    all_gather x1, waiting for transfers between devices, on_device(): residual_strip = lax.all_gather(cycle, 'row', axis=0, tiled=True)  63.3 us
    all_to_all x1, waiting for transfers between devices, on_device(): lax.all_to_all(residual_strip, 'col', split_axis=0, concat_axis=1, tiled=...  36.4 us
    reshape x1, local copies, waits for them, and re-layouts, on_device(): piece.reshape(occ_row, piece_count, slot_count, tile_width, tile_width)  17.9 us
    another operation x1, local copies, waits for them, and re-layouts, on_device(): received.reshape(piece_count, occ_col, slot_count, tile_width, tile_width)  11.1 us
    dot_general x1, matrix products, on_device(): jnp.einsum('iksac,kjscb->ijsab', left_tiles, right_tiles, preferred_eleme...  11.1 us
    all_gather x1, local copies, waits for them, and re-layouts, on_device(): piece = lax.all_gather(amplitudes, 'col', axis=1, tiled=True)  9.35 us
    gather x1, local copies, waits for them, and re-layouts, on_device(): packed = jnp.take(integrals, tile_second.reshape(-1), axis=2)  8.51 us
  transfers between devices with their start and end apart: 4, of which 3 were waited for; matrix products, arithmetic and copies ran while one was open for 10% of the time, Pallas kernels for 0%

commit v1 on v0

--- a/solution.py
+++ b/solution.py
@@ -4,6 +4,16 @@
 from jax.sharding import PartitionSpec as P
 
 TILE = 64
+
+
+def mirror_pairs(row_devices, col_devices, step):
+    ratio = col_devices // row_devices
+    pairs = []
+    for row in range(row_devices):
+        for col in range(col_devices):
+            part = (col % ratio + step) % ratio
+            pairs.append((row * col_devices + col, (col // ratio) * col_devices + row * ratio + part))
+    return pairs
 
 
 def on_device(amplitudes, integrals, pair_lists, tile_counts):
@@ -32,9 +42,17 @@
     live_slots = (jnp.arange(slot_count, dtype=jnp.int32) < my_count).astype(jnp.float32)
     cycle_value = (cycle_sum * live_slots[None, None, :, None, None]).astype(jnp.bfloat16)
     cycle = cycle_value.reshape(occ_row, occ_col, slot_count, square)
-    residual_strip = lax.all_gather(cycle, "row", axis=0, tiled=True)
-    mirror_whole = lax.all_to_all(residual_strip, "col", split_axis=0, concat_axis=1, tiled=True)
-    mirror_block = lax.dynamic_slice_in_dim(mirror_whole, my_row * occ_row, occ_row, 1)
+    halves = cycle.reshape(col_ratio, occ_col, occ_col, slot_count, square)
+    col_part = lax.rem(my_col, col_ratio)
+    arrived = []
+    for step in range(col_ratio):
+        part = lax.rem(col_part + step, col_ratio)
+        block = lax.dynamic_index_in_dim(halves, part, 0, keepdims=False)
+        arrived.append(lax.ppermute(block, ("row", "col"), mirror_pairs(row_devices, col_devices, step)))
+    arrived = jnp.stack(arrived)
+    order = lax.rem(col_part - jnp.arange(col_ratio) + col_ratio, col_ratio)
+    arrived = jnp.take(arrived, order, axis=0)
+    mirror_block = jnp.moveaxis(arrived, 0, 1).reshape(occ_col, occ_row, slot_count, square)
     mirror_block = mirror_block.reshape(occ_col, occ_row, slot_count, tile_width, tile_width)
     mine_first = lax.dynamic_index_in_dim(tile_first, my_row, 0, keepdims=False)
     mine_second = lax.dynamic_index_in_dim(tile_second, my_row, 0, keepdims=False)

time: 290 us -> 236 us (0.81)
  waiting for transfers between devices: 168 us -> 118 us
    all_gather x1 -> x0, waiting for transfers between devices: 63.3 us -> none  [on_device(): residual_strip = lax.all_gather(cycle, 'row', axis=0, tiled=True)]
    ppermute x0 -> x2, waiting for transfers between devices: none -> 48.5 us  [on_device(): lax.ppermute(block, ('row', 'col'), mirror_pairs(row_devices, col_devices...]
    all_to_all x1 -> x0, waiting for transfers between devices: 36.4 us -> none  [on_device(): lax.all_to_all(residual_strip, 'col', split_axis=0, concat_axis=1, tiled=...]
    ppermute x0 -> x2, starting transfers between devices: none -> 5.91 us  [on_device(): lax.ppermute(block, ('row', 'col'), mirror_pairs(row_devices, col_devices...]
    all_to_all x1 -> x0, starting transfers between devices: 5.34 us -> none  [on_device(): lax.all_to_all(residual_strip, 'col', split_axis=0, concat_axis=1, tiled=...]
    all_to_all x1 -> x0, local copies, waits for them, and re-layouts: 5.13 us -> none  [on_device(): lax.all_to_all(residual_strip, 'col', split_axis=0, concat_axis=1, tiled=...]
    reshape x2 -> x0, local copies, waits for them, and re-layouts: 4.87 us -> none  [the longest x1 3.85 us: on_device(): cycle = cycle_value.reshape(occ_row, occ_col, slot_count, square)]
    another operation x0 -> x2, local copies, waits for them, and re-layouts: none -> 4.1 us  [the longest x1 3.08 us: on_device(): halves = cycle.reshape(col_ratio, occ_col, occ_col, slot_count, square)]
  transfers between devices with their start and end apart: 4 -> 4, of which waited for: 3 -> 3; matrix products, arithmetic and copies ran while one was open for 10% -> 12% of each run, Pallas kernels for 0% -> 0%
where the time goes in v1:
time: 236 us; the launch traced here: 235 us
  waiting for transfers between devices  118 us (50%)
  local copies, waits for them, and re-layouts  68.9 us (29%)
  between operations  13.6 us (6%)
  matrix products  12.2 us (5%)
  other arithmetic  11.9 us (5%)
  starting transfers between devices  10.9 us (5%)
    all_to_all x1, waiting for transfers between devices, on_device(): lax.all_to_all(packed, 'row', split_axis=2, concat_axis=0, tiled=True)  69 us
    ppermute x2, waiting for transfers between devices, on_device(): lax.ppermute(block, ('row', 'col'), mirror_pairs(row_devices, col_devices...  48.5 us
    reshape x1, local copies, waits for them, and re-layouts, on_device(): piece.reshape(occ_row, piece_count, slot_count, tile_width, tile_width)  17.9 us
    another operation x1, local copies, waits for them, and re-layouts, on_device(): received.reshape(piece_count, occ_col, slot_count, tile_width, tile_width)  11.1 us
    dot_general x1, matrix products, on_device(): jnp.einsum('iksac,kjscb->ijsab', left_tiles, right_tiles, preferred_eleme...  11.1 us
    all_gather x1, local copies, waits for them, and re-layouts, on_device(): piece = lax.all_gather(amplitudes, 'col', axis=1, tiled=True)  9.34 us
    gather x1, local copies, waits for them, and re-layouts, on_device(): packed = jnp.take(integrals, tile_second.reshape(-1), axis=2)  8.5 us
    select_n x2, other arithmetic, on_device(): packed = jnp.take(integrals, tile_second.reshape(-1), axis=2)  6.63 us
  transfers between devices with their start and end apart: 4, of which 3 were waited for; matrix products, arithmetic and copies ran while one was open for 12% of the time, Pallas kernels for 0%

profile of v1, /device:TPU:3, one launch (start us, length us, event | category | flops | bytes accessed | tf_op | source)
XLA Modules:
  0.0 234.9 jit_solution(8737630853103244513)
XLA Ops:
  6.5 0.0 copy-start
  6.5 0.0 all-gather.2.cloned.1.call-start
  6.5 2.8 %copy.23 = bf16[4,2,12,4096]{3,0,2,1:T(4,128)(2,1)} copy(bf16[4,2,12,4096]{3,1,2,0:T(2,128)(2,1)} %param.4) | data formatting | bytes 1572864 | tf_op args[0]
  9.3 0.0 all-gather.2.cloned.1.call-update
  9.3 0.8 fusion.33
  10.1 0.1 reshape_squeeze.6
  10.2 0.0 copy-done
  10.2 8.5 %gather_fusion = bf16[48,4,2,4096]{3,2,1,0:T(2,128)(2,1)} fusion(bf16[4,2,47,4096]{3,1,2,0:T(2,128)(2,1)S(1)} %copy-done, s32[1024]{0:T(1024)S(1)} %pad_clamp_fusion.1), kind=kCustom, calls=%fused_computation | custom fusion | bytes 6291648 | tf_op jit(solution)/shard_map/jit(_take)/gather | solution.py:30
  18.7 6.6 %broadcast_select_fusion = bf16[4,2,4,12,4096]{4,1,3,0,2:T(2,128)(2,1)} fusion(pred[4,12]{1,0:T(4,128)(4,1)S(1)} %compare_and_fusion.1, bf16[4,2,4,12,4096]{4,1,0,3,2:T(2,128)(2,1)} %bitcast.73), kind=kLoop, calls=%fused_computation.5 | loop fusion | flops 1572864 | bytes 6291504 | tf_op jit(solution)/shard_map/jit(_take)/select_n | solution.py:30
  25.4 0.0 copy-start.4
  25.4 5.0 %all-to-all-start = ((bf16[4,2,4,12,4096]{4,1,3,0,2:T(2,128)(2,1)}), bf16[4,2,4,12,4096]{4,1,3,0,2:T(2,128)(2,1)}, u32[]{:S(2)}, u32[]{:S(2)}) async-start(bf16[4,2,4,12,4096]{4,1,3,0,2:T(2,128)(2,1)} %broadcast_select_fusion), calls=%async_computation | async-start | bytes 6291456 | tf_op jit(solution)/shard_map/all_to_all | solution.py:32
  30.4 0.0 copy-done.4
  30.4 0.6 dynamic_slice.24
  31.0 0.6 compare_convert_fusion
  31.6 69.0 %all-to-all-done = bf16[4,2,4,12,4096]{4,1,3,0,2:T(2,128)(2,1)} async-done(((bf16[4,2,4,12,4096]{4,1,3,0,2:T(2,128)(2,1)}), bf16[4,2,4,12,4096]{4,1,3,0,2:T(2,128)(2,1)}, u32[]{:S(2)}, u32[]{:S(2)}) %all-to-all-start) | async-done | bytes 3145760 | tf_op jit(solution)/shard_map/all_to_all | solution.py:32
  100.6 11.1 %reshape_reshape.9 = bf16[16,2,12,64,64]{4,3,1,2,0:T(8,128)(2,1)} reshape(bf16[4,4,2,1,12,4096]{5,2,4,1,0,3:T(2,128)(2,1)} %bitcast.5) | data formatting | bytes 6291456 | tf_op jit(solution)/shard_map/reshape;reshape | solution.py:37
  111.7 0.0 all-gather.2.cloned.1.call-done
  111.7 9.3 %copy.24 = bf16[4,16,12,4096]{3,1,0,2:T(8,128)(2,1)} copy(bf16[4,16,12,4096]{3,0,2,1:T(4,128)(2,1)} %all-gather.2.cloned.1.call-done) | data formatting | bytes 12582912 | tf_op jit(solution)/shard_map/all_gather | solution.py:34
  121.1 17.9 %reshape.123 = bf16[4,16,12,64,64,1]{4,3,1,0,2,5:T(8,128)(2,1)} reshape(bf16[4,16,12,4096]{3,1,0,2:T(8,128)(2,1)} %copy.24) | data formatting | bytes 12582912 | tf_op jit(solution)/shard_map/reshape | solution.py:36
  139.0 11.1 %fusion.11 = bf16[4,2,12,64,64]{3,4,0,1,2:T(8,128)(2,1)S(1)} fusion(f32[12]{0:T(128)S(1)} %compare_convert_fusion, bf16[4,16,12,64,64,1]{4,3,1,0,2,5:T(8,128)(2,1)} %reshape.123, bf16[16,2,12,64,64]{4,3,1,2,0:T(8,128)(2,1)} %reshape_reshape.9), kind=kOutput, calls=%fused_computation.13 | convolution fusion | flops 806092800 | bytes 10223664 | tf_op jit(solution)/shard_map/iksac,kjscb->ijsab/dot_general | solution.py:38
  150.1 0.0 copy-start.2
  150.1 1.7 copy.26
  151.8 3.1 %reshape_reshape.10 = bf16[2,2,2,12,4096]{4,2,3,1,0:T(2,128)(2,1)S(1)} reshape(bf16[4,2,12,64,64]{4,3,1,2,0:T(8,128)(2,1)} %copy.26) | data formatting | bytes 1572864 | tf_op jit(solution)/shard_map/reshape;reshape | solution.py:45
  154.9 0.8 dynamic-slice_bitcast_fusion.1
  155.7 0.0 copy-done.2
  155.7 0.1 collective-permute-start.1
  155.8 5.8 %collective-permute-start = (bf16[2,2,12,4096]{3,1,2,0:T(2,128)(2,1)S(1)}, bf16[2,2,12,4096]{3,1,2,0:T(2,128)(2,1)S(1)}, u32[]{:S(2)}, u32[]{:S(2)}) collective-permute-start(bf16[2,2,12,4096]{3,1,2,0:T(2,128)(2,1)S(1)} %get-tuple-element.5), channel_id=1, source_target_pairs={{0,0},{1,1},{2,8},{3,9},{4,16},{5,17},{6,24},{7,25},{8,2},{9,3},{1... | collective-permute-start | bytes 1179656 | tf_op jit(solution)/shard_map/ppermute | solution.py:51
  161.7 39.6 %collective-permute-done.1 = bf16[2,2,12,4096]{3,1,2,0:T(2,128)(2,1)S(1)} collective-permute-done((bf16[2,2,12,4096]{3,1,2,0:T(2,128)(2,1)S(1)}, bf16[2,2,12,4096]{3,1,2,0:T(2,128)(2,1)S(1)}, u32[]{:S(2)}, u32[]{:S(2)}) %collective-permute-start.1) | collective-permute-done | bytes 393248 | tf_op jit(solution)/shard_map/ppermute | solution.py:51
  201.3 8.9 %collective-permute-done = bf16[2,2,12,4096]{3,1,2,0:T(2,128)(2,1)S(1)} collective-permute-done((bf16[2,2,12,4096]{3,1,2,0:T(2,128)(2,1)S(1)}, bf16[2,2,12,4096]{3,1,2,0:T(2,128)(2,1)S(1)}, u32[]{:S(2)}, u32[]{:S(2)}) %collective-permute-start) | collective-permute-done | bytes 393248 | tf_op jit(solution)/shard_map/ppermute | solution.py:51
  210.2 1.1 pad_maximum_fusion
  211.3 2.1 gather_fusion.1
  213.5 0.7 fusion.16
  214.2 0.8 copy.27
  215.0 1.0 reshape_reshape.11
  216.1 0.0 copy-start.3
  216.1 1.1 fusion.5
  217.2 0.3 copy-done.3
  217.5 2.7 %fusion.3 = f32[4,2,12,64,64]{3,4,0,1,2:T(8,128)} fusion(f32[2,4,64,64,12]{3,4,2,1,0:T(8,128)S(1)} %fusion.5, bf16[4,2,12,64,64]{3,4,0,1,2:T(8,128)(2,1)S(1)} %copy-done.3, f32[12]{0:T(128)S(1)} %compare_convert_fusion), kind=kLoop, calls=%fused_computation.7 | loop fusion | flops 1179648 | bytes 3932208 | tf_op jit(solution)/shard_map/mul | solution.py:69
  220.2 0.0 copy-start.1
  220.2 3.7 %copy.30 = f32[4,2,12,64,64]{4,3,1,2,0:T(8,128)} copy(f32[4,2,12,64,64]{3,4,0,1,2:T(8,128)} %fusion.3) | data formatting | bytes 3145728 | tf_op jit(solution)/shard_map/mul | solution.py:69
  223.9 4.2 %reshape.105 = f32[4,2,12,4096]{3,1,2,0:T(2,128)} reshape(f32[4,2,12,64,64]{4,3,1,2,0:T(8,128)} %copy.30) | data formatting | bytes 3145728 | tf_op jit(solution)/shard_map/reshape | solution.py:70
  228.1 0.0 copy-done.1
  (7 shorter events, 0.1 us)
Async XLA Ops:
  6.5 3.7 %copy-start = (bf16[4,2,47,4096]{3,1,2,0:T(2,128)(2,1)S(1)}, bf16[4,2,47,4096]{3,1,2,0:T(2,128)(2,1)}, u32[]{:S(2)}) copy-start(bf16[4,2,47,4096]{3,1,2,0:T(2,128)(2,1)} %param.5) | copy-start | bytes 9240580
  6.5 105.2 %all-gather.2.cloned.1.call-start = ((), (), s32[]{:S(2)}) async-start(), calls=%async_computation.1 | async-start | bytes 7077888 | tf_op jit(solution)/shard_map/all_gather | solution.py:34
  25.4 5.0 %copy-start.4 = (s32[4]{0:T(128)S(1)}, s32[4]{0:T(128)}, u32[]{:S(2)}) copy-start(s32[4]{0:T(128)} %param.7) | copy-start | bytes 52
  25.4 75.3 %all-to-all-start = ((bf16[4,2,4,12,4096]{4,1,3,0,2:T(2,128)(2,1)}), bf16[4,2,4,12,4096]{4,1,3,0,2:T(2,128)(2,1)}, u32[]{:S(2)}, u32[]{:S(2)}) async-start(bf16[4,2,4,12,4096]{4,1,3,0,2:T(2,128)(2,1)} %broadcast_select_fusion), calls=%async_computation | async-start | bytes 6291456 | tf_op jit(solution)/shard_map/all_to_all | solution.py:32
  150.1 5.6 %copy-start.2 = (bf16[4,2,12,64,64]{3,4,0,1,2:T(8,128)(2,1)}, bf16[4,2,12,64,64]{3,4,0,1,2:T(8,128)(2,1)S(1)}, u32[]{:S(2)}) copy-start(bf16[4,2,12,64,64]{3,4,0,1,2:T(8,128)(2,1)S(1)} %fusion.11) | copy-start | bytes 2359300
  155.7 45.6 %collective-permute-start.1 = (bf16[2,2,12,4096]{3,1,2,0:T(2,128)(2,1)S(1)}, bf16[2,2,12,4096]{3,1,2,0:T(2,128)(2,1)S(1)}, u32[]{:S(2)}, u32[]{:S(2)}) collective-permute-start(bf16[2,2,12,4096]{3,1,2,0:T(2,128)(2,1)S(1)} %get-tuple-element.6), channel_id=1, source_target_pairs={{0,1},{1,0},{2,9},{3,8},{4,17},{5,16},{6,25},{7,24},{8,3},{9,2},{1... | collective-permute-start | bytes 1179656 | tf_op jit(solution)/shard_map/ppermute | solution.py:51
  155.8 54.4 %collective-permute-start = (bf16[2,2,12,4096]{3,1,2,0:T(2,128)(2,1)S(1)}, bf16[2,2,12,4096]{3,1,2,0:T(2,128)(2,1)S(1)}, u32[]{:S(2)}, u32[]{:S(2)}) collective-permute-start(bf16[2,2,12,4096]{3,1,2,0:T(2,128)(2,1)S(1)} %get-tuple-element.5), channel_id=1, source_target_pairs={{0,0},{1,1},{2,8},{3,9},{4,16},{5,17},{6,24},{7,25},{8,2},{9,3},{1... | collective-permute-start | bytes 1179656 | tf_op jit(solution)/shard_map/ppermute | solution.py:51
  216.1 1.4 copy-start.3
  220.2 7.9 %copy-start.1 = (bf16[4,2,47,4096]{3,1,2,0:T(2,128)(2,1)S(1)}, bf16[4,2,47,4096]{3,1,2,0:T(2,128)(2,1)}, u32[]{:S(2)}) copy-start(bf16[4,2,47,4096]{3,1,2,0:T(2,128)(2,1)} %param.5) | copy-start | bytes 9240580
Sparse Core Ops, SparseCore 0:
  9.5 47.0 all-gather.1
